TPU v7x, 32 devices: a whole 2x2x4 slice. The times are simulated.
32 devices in a mesh: blk: 8 (over y, x, core), fsdp: 4 (over z).
Axes of the slice: x: 2, y: 2, z: 4, core: 2. Of those that a mesh axis runs over, the one named last changes fastest.
Arguments:
- hidden: bfloat16 [8, 512, 5120], P('blk', 'fsdp'), may hold values from -6 to 6
- grad_query: bfloat16 [8, 512, 5120], P('blk', 'fsdp'), may hold values from -6 to 6
- grad_value: bfloat16 [8, 512, 5120], P('blk', 'fsdp'), may hold values from -6 to 6
- adapters: bfloat16 [8, 192, 5120], P('blk', 'fsdp'), may hold values from -4 to 4
- first_moment: bfloat16 [8, 192, 5120], P('blk', 'fsdp'), may hold values from -0.009765625 to 0.009765625
- second_moment: bfloat16 [8, 192, 5120], P('blk', 'fsdp'), may hold values from 8.090865e-09 to 8.1025064e-08
- mixing: int32 [8, 3], P('blk'), may hold values from 1 to 2, as said below
Outputs:
- mixed: bfloat16 [8, 192, 5120], P('blk', 'fsdp')
Inputs may be any that keep to these rules, and one draw needn't show every extreme that they name: `mixing`: each row holds two numerators equal to 1 and one equal to 2.
All inputs are finite; a program needn't handle non-finite values.
Results may differ from a plain program's by a relative error of at most 0.0051.
Values may be sent and summed in bfloat16 or wider, within the bound.
A program may use at most 64 MiB of HBM per device.

v0:
```python
import math
import jax
import jax.numpy as jnp
from jax import lax
from jax.sharding import PartitionSpec as P

beta_one = 0.9
beta_two = 0.999
learn_rate = 0.2
decay_rate = 0.5
epsilon = 1e-08


def shifted(array, axis, by):
    length = lax.axis_size(axis)
    return lax.ppermute(array, axis, [(i, (i + by) % length) for i in range(length)])


def contract_tokens(left, right, scale):
    return (
        lax.dot_general(left, right, (((0,), (0,)), ((), ())), preferred_element_type=jnp.float32)
        * scale
    )


def shards(hidden, grad_query, grad_value, adapters, first_moment, second_moment, mixing):
    tokens = hidden[0]
    width = tokens.shape[1]
    full_rows = lax.all_gather(adapters, "fsdp", axis=1, tiled=True)[0]
    rank = full_rows.shape[0] // 4
    inv_width = 1.0 / math.sqrt(width)
    inv_rank = 1.0 / math.sqrt(rank)
    factors = []
    for index, cot in ((0, grad_query[0]), (1, grad_value[0])):
        down = full_rows[2 * index * rank : (2 * index + 1) * rank]
        up_rows = full_rows[(2 * index + 1) * rank : (2 * index + 2) * rank]
        lowrank = (jnp.dot(tokens, down.T, preferred_element_type=jnp.float32) * inv_width).astype(
            jnp.bfloat16
        )
        back = (jnp.dot(cot, up_rows.T, preferred_element_type=jnp.float32) * inv_rank).astype(
            jnp.bfloat16
        )
        factors.append((back, tokens, inv_width))
        factors.append((lowrank, cot, inv_rank))
    shard_rows = adapters.shape[1]
    group_tokens = tokens.shape[0] * lax.axis_size("fsdp")
    weights = mixing[0].astype(jnp.float32)
    term = jnp.concatenate(
        [contract_tokens(left, right, scale) for left, right, scale in factors], axis=0
    )

    def owned_rows(start, count, term=term):
        return term

    gradient = (
        lax.psum_scatter(
            owned_rows(jnp.int32(0), lax.axis_size("fsdp") * shard_rows).astype(jnp.bfloat16),
            "fsdp",
            scatter_dimension=0,
            tiled=True,
        ).astype(jnp.float32)
        / group_tokens
    )
    params = adapters[0].astype(jnp.float32)
    first = first_moment[0].astype(jnp.float32)
    second = second_moment[0].astype(jnp.float32)
    new_first = beta_one * first + (1.0 - beta_one) * gradient
    new_second = beta_two * second + (1.0 - beta_two) * gradient * gradient
    first_hat = new_first / (1.0 - beta_one**2)
    second_hat = new_second / (1.0 - beta_two**2)
    step = first_hat / (jnp.sqrt(second_hat) + epsilon) + decay_rate * params
    updated = (params - learn_rate * step).astype(jnp.bfloat16)
    lower = shifted(updated, "blk", 1)
    upper = shifted(updated, "blk", -1)
    total = weights[0] * lower.astype(jnp.float32) + weights[1] * updated.astype(jnp.float32)
    total = total + weights[2] * upper.astype(jnp.float32)
    results = (total / 4.0).astype(jnp.bfloat16)
    return results[None]


def solution(mesh):
    in_specs = (
        P("blk", "fsdp", None),
        P("blk", "fsdp", None),
        P("blk", "fsdp", None),
        P("blk", "fsdp", None),
        P("blk", "fsdp", None),
        P("blk", "fsdp", None),
        P("blk", None),
    )
    out_specs = P("blk", "fsdp", None)
    return jax.shard_map(shards, mesh=mesh, in_specs=in_specs, out_specs=out_specs, check_vma=False)
```

profile of v0, /device:TPU:1, one launch (start us, length us, event | category | flops | bytes accessed | tf_op | source)
XLA Modules:
  0.0 135.9 jit_solution(4167797149082029256)
XLA Ops:
  6.5 0.0 copy-start
  6.5 0.0 all-gather.2.cloned.1.call-start
  6.5 0.7 all-gather.2.cloned.1.call-update
  7.3 0.0 copy-start.1
  7.3 0.0 reduce-scatter.2.cloned.1.call-start
  7.3 47.3 %all-gather.2.cloned.1.call-done = bf16[1,192,5120]{2,1,0:T(8,128)(2,1)} async-done(((bf16[1,48,5120]{2,1,0:T(8,128)(2,1)}), bf16[1,192,5120]{2,1,0:T(8,128)(2,1)}) %all-gather.2.cloned.1.call-update) | async-done | bytes 1966096 | tf_op jit(solution)/shard_map/all_gather | solution.py:29
  54.6 0.0 copy-done
  54.6 2.5 %fusion = bf16[48,5120]{1,0:T(8,128)(2,1)S(1)} fusion(bf16[1,128,5120]{2,1,0:T(8,128)(2,1)S(1)} %copy-done, bf16[1,128,5120]{2,1,0:T(8,128)(2,1)} %param.8, bf16[1,192,5120]{2,1,0:T(8,128)(2,1)} %all-gather.2.cloned.1.call-done), kind=kOutput, calls=%fused_computation.4 | convolution fusion | flops 126332928 | bytes 3604480 | tf_op jit(solution)/shard_map/dot_general | solution.py:21
  57.2 0.0 copy-done.1
  57.2 2.9 %fusion.1 = bf16[48,5120]{1,0:T(8,128)(2,1)} fusion(bf16[1,128,5120]{2,1,0:T(8,128)(2,1)S(1)} %copy-done.1, bf16[1,128,5120]{2,1,0:T(8,128)(2,1)S(1)} %copy-done, bf16[1,192,5120]{2,1,0:T(8,128)(2,1)} %all-gather.2.cloned.1.call-done), kind=kOutput, calls=%fused_computation.5 | convolution fusion | flops 126332928 | bytes 3604480 | tf_op jit(solution)/shard_map/dot_general | solution.py:21
  60.1 0.0 copy-start.2
  60.1 3.4 %fusion.2 = bf16[48,5120]{1,0:T(8,128)(2,1)} fusion(bf16[1,128,5120]{2,1,0:T(8,128)(2,1)S(1)} %copy-done, bf16[1,128,5120]{2,1,0:T(8,128)(2,1)} %param.9, bf16[1,192,5120]{2,1,0:T(8,128)(2,1)} %all-gather.2.cloned.1.call-done), kind=kOutput, calls=%fused_computation.6 | convolution fusion | flops 126332928 | bytes 3604480 | tf_op jit(solution)/shard_map/dot_general | solution.py:21
  63.6 0.0 copy-done.2
  63.6 2.9 %fusion.3 = bf16[48,5120]{1,0:T(8,128)(2,1)} fusion(bf16[1,128,5120]{2,1,0:T(8,128)(2,1)S(1)} %copy-done.2, bf16[1,128,5120]{2,1,0:T(8,128)(2,1)S(1)} %copy-done, bf16[1,192,5120]{2,1,0:T(8,128)(2,1)} %all-gather.2.cloned.1.call-done), kind=kOutput, calls=%fused_computation.7 | convolution fusion | flops 126332928 | bytes 3604480 | tf_op jit(solution)/shard_map/dot_general | solution.py:21
  66.5 2.8 %pad_maximum_fusion = bf16[192,5120]{1,0:T(8,128)(2,1)} fusion(bf16[48,5120]{1,0:T(8,128)(2,1)} %fusion.3, bf16[48,5120]{1,0:T(8,128)(2,1)} %fusion.2, bf16[48,5120]{1,0:T(8,128)(2,1)} %fusion.1, bf16[48,5120]{1,0:T(8,128)(2,1)S(1)} %fusion), kind=kLoop, calls=%fused_computation.8 | loop fusion | flops 7864320 | bytes 3932160 | tf_op jit(solution)/shard_map/concatenate | solution.py:48
  69.2 0.0 copy-start.3
  69.2 0.0 copy-start.4
  69.2 0.0 copy-start.5
  69.2 0.0 reduce-scatter.2.cloned.1.call-update
  69.3 0.0 copy-start.6
  69.3 40.3 %reduce-scatter.2.cloned.1.call-done = bf16[48,5120]{1,0:T(8,128)(2,1)} async-done(((bf16[192,5120]{1,0:T(8,128)(2,1)}), bf16[48,5120]{1,0:T(8,128)(2,1)}) %reduce-scatter.2.cloned.1.call-update) | async-done | bytes 491536 | tf_op jit(solution)/shard_map/reduce_scatter | solution.py:56
  109.5 0.0 copy-done.3
  109.5 0.0 copy-done.4
  109.5 0.0 copy-done.5
  109.5 1.9 %fusion.50 = bf16[48,5120]{1,0:T(8,128)(2,1)S(1)} fusion(bf16[48,5120]{1,0:T(8,128)(2,1)} %reduce-scatter.2.cloned.1.call-done, bf16[1,48,5120]{2,1,0:T(8,128)(2,1)S(1)} %copy-done.4, bf16[1,48,5120]{2,1,0:T(8,128)(2,1)S(1)} %copy-done.5, bf16[1,48,5120]{2,1,0:T(8,128)(2,1)S(1)} %copy-done.3), kind=kLoop, calls=%fused_computation.36 | loop fusion | flops 5160960 | bytes 2457600 | tf_op jit(solution)/shard_map/convert_element_type | solution.py:72
  111.5 2.0 %collective-permute-start = (bf16[48,5120]{1,0:T(8,128)(2,1)S(1)}, bf16[48,5120]{1,0:T(8,128)(2,1)S(1)}, u32[]{:S(2)}, u32[]{:S(2)}) collective-permute-start(bf16[48,5120]{1,0:T(8,128)(2,1)S(1)} %fusion.50), channel_id=1, source_target_pairs={{0,4},{4,8},{8,12},{12,16},{16,20},{20,24},{24,28},{28,0},{1,5},{5... | collective-permute-start | bytes 1474568 | tf_op jit(solution)/shard_map/ppermute | solution.py:16
  113.5 0.0 collective-permute-start.1
  113.5 0.0 copy-done.6
  113.5 0.6 fusion.68
  114.1 8.6 %collective-permute-done = bf16[48,5120]{1,0:T(8,128)(2,1)S(1)} collective-permute-done((bf16[48,5120]{1,0:T(8,128)(2,1)S(1)}, bf16[48,5120]{1,0:T(8,128)(2,1)S(1)}, u32[]{:S(2)}, u32[]{:S(2)}) %collective-permute-start) | collective-permute-done | bytes 491552 | tf_op jit(solution)/shard_map/ppermute | solution.py:16
  122.7 3.5 %collective-permute-done.1 = bf16[48,5120]{1,0:T(8,128)(2,1)S(1)} collective-permute-done((bf16[48,5120]{1,0:T(8,128)(2,1)S(1)}, bf16[48,5120]{1,0:T(8,128)(2,1)S(1)}, u32[]{:S(2)}, u32[]{:S(2)}) %collective-permute-start.1) | collective-permute-done | bytes 491552 | tf_op jit(solution)/shard_map/ppermute | solution.py:16
  126.1 2.9 %fusion.59 = bf16[1,48,5120]{2,1,0:T(8,128)(2,1)} fusion(bf16[48,5120]{1,0:T(8,128)(2,1)S(1)} %collective-permute-done.1, bf16[48,5120]{1,0:T(8,128)(2,1)S(1)} %fusion.50, bf16[48,5120]{1,0:T(8,128)(2,1)S(1)} %collective-permute-done, f32[]{:T(128)} %bitcast.13, f32[]{:T(128)} %bitcast.12, f32[]{:T(128)} %bitcast), kind=kLoop, calls=%fused_computation.46 | loop fusion | flops 2457600 | bytes 1966092 | tf_op jit(solution)/shard_map/broadcast_in_dim | solution.py:78
  (1 shorter events, 0.0 us)
Async XLA Ops:
  6.5 48.1 %copy-start = (bf16[1,128,5120]{2,1,0:T(8,128)(2,1)S(1)}, bf16[1,128,5120]{2,1,0:T(8,128)(2,1)}, u32[]{:S(2)}) copy-start(bf16[1,128,5120]{2,1,0:T(8,128)(2,1)} %param.7) | copy-start | bytes 3932164
  6.5 48.1 %all-gather.2.cloned.1.call-start = ((), (), s32[]{:S(2)}) async-start(), calls=%async_computation.1 | async-start | bytes 2457600 | tf_op jit(solution)/shard_map/all_gather | solution.py:29
  7.3 49.9 %copy-start.1 = (bf16[1,128,5120]{2,1,0:T(8,128)(2,1)S(1)}, bf16[1,128,5120]{2,1,0:T(8,128)(2,1)}, u32[]{:S(2)}) copy-start(bf16[1,128,5120]{2,1,0:T(8,128)(2,1)} %param.8) | copy-start | bytes 3932164
  7.3 102.3 %reduce-scatter.2.cloned.1.call-start = ((), (), s32[]{:S(2)}) async-start(), calls=%async_computation.2 | async-start | bytes 2457600 | tf_op jit(solution)/shard_map/reduce_scatter | solution.py:56
  60.1 3.4 %copy-start.2 = (bf16[1,128,5120]{2,1,0:T(8,128)(2,1)S(1)}, bf16[1,128,5120]{2,1,0:T(8,128)(2,1)}, u32[]{:S(2)}) copy-start(bf16[1,128,5120]{2,1,0:T(8,128)(2,1)} %param.9) | copy-start | bytes 3932164
  69.2 40.3 %copy-start.3 = (bf16[1,48,5120]{2,1,0:T(8,128)(2,1)S(1)}, bf16[1,48,5120]{2,1,0:T(8,128)(2,1)}, u32[]{:S(2)}) copy-start(bf16[1,48,5120]{2,1,0:T(8,128)(2,1)} %param.10) | copy-start | bytes 1474564
  69.2 40.3 %copy-start.4 = (bf16[1,48,5120]{2,1,0:T(8,128)(2,1)S(1)}, bf16[1,48,5120]{2,1,0:T(8,128)(2,1)}, u32[]{:S(2)}) copy-start(bf16[1,48,5120]{2,1,0:T(8,128)(2,1)} %param.12) | copy-start | bytes 1474564
  69.2 40.3 %copy-start.5 = (bf16[1,48,5120]{2,1,0:T(8,128)(2,1)S(1)}, bf16[1,48,5120]{2,1,0:T(8,128)(2,1)}, u32[]{:S(2)}) copy-start(bf16[1,48,5120]{2,1,0:T(8,128)(2,1)} %param.11) | copy-start | bytes 1474564
  69.3 44.2 %copy-start.6 = (s32[1,3]{1,0:T(1,128)S(1)}, s32[1,3]{1,0:T(1,128)}, u32[]{:S(2)}) copy-start(s32[1,3]{1,0:T(1,128)} %param.13) | copy-start | bytes 40
  111.5 11.2 %collective-permute-start = (bf16[48,5120]{1,0:T(8,128)(2,1)S(1)}, bf16[48,5120]{1,0:T(8,128)(2,1)S(1)}, u32[]{:S(2)}, u32[]{:S(2)}) collective-permute-start(bf16[48,5120]{1,0:T(8,128)(2,1)S(1)} %fusion.50), channel_id=1, source_target_pairs={{0,4},{4,8},{8,12},{12,16},{16,20},{20,24},{24,28},{28,0},{1,5},{5... | collective-permute-start | bytes 1474568 | tf_op jit(solution)/shard_map/ppermute | solution.py:16
  113.5 12.7 %collective-permute-start.1 = (bf16[48,5120]{1,0:T(8,128)(2,1)S(1)}, bf16[48,5120]{1,0:T(8,128)(2,1)S(1)}, u32[]{:S(2)}, u32[]{:S(2)}) collective-permute-start(bf16[48,5120]{1,0:T(8,128)(2,1)S(1)} %fusion.50), channel_id=1, source_target_pairs={{0,28},{4,0},{8,4},{12,8},{16,12},{20,16},{24,20},{28,24},{1,29},{... | collective-permute-start | bytes 1474568 | tf_op jit(solution)/shard_map/ppermute | solution.py:16
Sparse Core Ops, SparseCore 0:
  8.9 45.6 all-gather.1
  69.4 40.0 reduce-scatter.1
where the time goes:
time: 136 us
  waiting for transfers between devices  100 us (74%)
  between operations  13.4 us (10%)
  matrix products  11.9 us (9%)
  other arithmetic  7.59 us (6%)
  starting transfers between devices  2.01 us (1%)
    all_gather x1, waiting for transfers between devices, shards(): full_rows = lax.all_gather(adapters, 'fsdp', axis=1, tiled=True)[0]  47.3 us
    reduce_scatter x1, waiting for transfers between devices, shards(): lax.psum_scatter(owned_rows(jnp.int32(0), lax.axis_size('fsdp') * shard_r...  40.3 us
    ppermute x2, waiting for transfers between devices, shifted(): lax.ppermute(array, axis, [(i, (i + by) % length) for i in range(length)])  12 us
    dot_general x4, matrix products, contract_tokens(): lax.dot_general(left, right, (((0,), (0,)), ((), ())), preferred_element_...  11.9 us
    broadcast_in_dim x1, other arithmetic, shards(): return results[None]  2.89 us
    concatenate x1, other arithmetic, shards(): jnp.concatenate([contract_tokens(left, right, scale) for left, right, sca...  2.75 us
  transfers between devices with their start and end apart: 4, of which 4 were waited for; matrix products, arithmetic and copies ran while one was open for 0% of the time, Pallas kernels for 0%

commit v1 on v0

--- a/solution.py
+++ b/solution.py
@@ -9,6 +9,19 @@
 learn_rate = 0.2
 decay_rate = 0.5
 epsilon = 1e-08
+
+
+def ring_gather(x, axis, dim):
+    size, position, rows = (lax.axis_size(axis), lax.axis_index(axis), x.shape[dim])
+    right = [(i, (i + 1) % size) for i in range(size)]
+    result = jnp.zeros((*x.shape[:dim], size * rows, *x.shape[dim + 1 :]), x.dtype)
+    held = x
+    for step in range(size):
+        owner = (position - step) % size
+        result = lax.dynamic_update_slice_in_dim(result, held, owner * rows, axis=dim)
+        if step < size - 1:
+            held = lax.ppermute(held, axis, right)
+    return result
 
 
 def shifted(array, axis, by):
@@ -26,7 +39,7 @@
 def shards(hidden, grad_query, grad_value, adapters, first_moment, second_moment, mixing):
     tokens = hidden[0]
     width = tokens.shape[1]
-    full_rows = lax.all_gather(adapters, "fsdp", axis=1, tiled=True)[0]
+    full_rows = ring_gather(adapters, "fsdp", 1)[0]
     rank = full_rows.shape[0] // 4
     inv_width = 1.0 / math.sqrt(width)
     inv_rank = 1.0 / math.sqrt(rank)

time: 136 us -> 132 us (0.971)
  waiting for transfers between devices: 100 us -> 90.4 us
  local copies, waits for them, and re-layouts: 0.68 us -> 2.9 us
  starting transfers between devices: 2.01 us -> 4.1 us
    all_gather x1 -> x0, waiting for transfers between devices: 47.3 us -> none  [shards(): full_rows = lax.all_gather(adapters, 'fsdp', axis=1, tiled=True)[0]]
    ppermute x0 -> x3, waiting for transfers between devices: none -> 36.8 us  [ring_gather(): held = lax.ppermute(held, axis, right)]
    ppermute x0 -> x3, starting transfers between devices: none -> 2.13 us  [ring_gather(): held = lax.ppermute(held, axis, right)]
  transfers between devices with their start and end apart: 4 -> 6, of which waited for: 4 -> 6; matrix products, arithmetic and copies ran while one was open for 0% -> 2% of each run, Pallas kernels for 0% -> 0%
where the time goes in v1:
time: 132 us; the launch traced here: 131 us
  waiting for transfers between devices  90.4 us (68%)
  between operations  13.5 us (10%)
  matrix products  12.8 us (10%)
  other arithmetic  7.74 us (6%)
  starting transfers between devices  4.1 us (3%)
  local copies, waits for them, and re-layouts  2.9 us (2%)
    reduce_scatter x1, waiting for transfers between devices, shards(): lax.psum_scatter(owned_rows(jnp.int32(0), lax.axis_size('fsdp') * shard_r...  41.6 us
    ppermute x3, waiting for transfers between devices, ring_gather(): held = lax.ppermute(held, axis, right)  36.8 us
    dot_general x4, matrix products, contract_tokens(): lax.dot_general(left, right, (((0,), (0,)), ((), ())), preferred_element_...  12.8 us
    ppermute x2, waiting for transfers between devices, shifted(): lax.ppermute(array, axis, [(i, (i + by) % length) for i in range(length)])  12 us
    broadcast_in_dim x1, other arithmetic, shards(): return results[None]  2.91 us
    concatenate x1, other arithmetic, shards(): jnp.concatenate([contract_tokens(left, right, scale) for left, right, sca...  2.89 us
  transfers between devices with their start and end apart: 6, of which 6 were waited for; matrix products, arithmetic and copies ran while one was open for 2% of the time, Pallas kernels for 0%

profile of v1, /device:TPU:1, one launch (start us, length us, event | category | flops | bytes accessed | tf_op | source)
XLA Modules:
  0.0 131.4 jit_solution(8146070024175631497)
XLA Ops:
  6.5 0.0 copy-start
  6.5 0.0 reduce-scatter.2.cloned.1.call-start
  6.5 2.1 %collective-permute-start = (bf16[1,48,5120]{2,1,0:T(8,128)(2,1)}, bf16[1,48,5120]{2,1,0:T(8,128)(2,1)}, u32[]{:S(2)}, u32[]{:S(2)}) collective-permute-start(bf16[1,48,5120]{2,1,0:T(8,128)(2,1)} %param.10), channel_id=1, source_target_pairs={{0,1},{1,2},{2,3},{3,0},{4,5},{5,6},{6,7},{7,4},{8,9},{9,10},{10,1... | collective-permute-start | bytes 1474568 | tf_op jit(solution)/shard_map/ppermute | solution.py:23
  8.7 0.0 copy-start.1
  8.7 0.2 squeeze.35
  8.9 0.9 copy-done.1
  9.8 12.1 %collective-permute-done = bf16[1,48,5120]{2,1,0:T(8,128)(2,1)} collective-permute-done((bf16[1,48,5120]{2,1,0:T(8,128)(2,1)}, bf16[1,48,5120]{2,1,0:T(8,128)(2,1)}, u32[]{:S(2)}, u32[]{:S(2)}) %collective-permute-start) | collective-permute-done | bytes 491552 | tf_op jit(solution)/shard_map/ppermute | solution.py:23
  22.0 0.0 collective-permute-start.1
  22.0 1.1 bitcast_dynamic-update-slice_fusion.2
  23.1 12.4 %collective-permute-done.1 = bf16[1,48,5120]{2,1,0:T(8,128)(2,1)S(1)} collective-permute-done((bf16[1,48,5120]{2,1,0:T(8,128)(2,1)}, bf16[1,48,5120]{2,1,0:T(8,128)(2,1)S(1)}, u32[]{:S(2)}, u32[]{:S(2)}) %collective-permute-start.1) | collective-permute-done | bytes 491552 | tf_op jit(solution)/shard_map/ppermute | solution.py:23
  35.4 0.0 collective-permute-start.2
  35.5 12.3 %collective-permute-done.2 = bf16[1,48,5120]{2,1,0:T(8,128)(2,1)S(1)} collective-permute-done((bf16[1,48,5120]{2,1,0:T(8,128)(2,1)S(1)}, bf16[1,48,5120]{2,1,0:T(8,128)(2,1)S(1)}, u32[]{:S(2)}, u32[]{:S(2)}) %collective-permute-start.2) | collective-permute-done | bytes 491552 | tf_op jit(solution)/shard_map/ppermute | solution.py:23
  47.9 0.0 copy-done
  47.9 3.2 %fusion = bf16[48,5120]{1,0:T(8,128)(2,1)} fusion(bf16[1,128,5120]{2,1,0:T(8,128)(2,1)S(1)} %copy-done, bf16[1,128,5120]{2,1,0:T(8,128)(2,1)} %param.8, bf16[192,5120]{1,0:T(8,128)(2,1)S(1)} %bitcast_dynamic-update-slice_fusion), kind=kOutput, calls=%fused_computation.4 | convolution fusion | flops 126332928 | bytes 3604480 | tf_op jit(solution)/shard_map/dot_general | solution.py:34
  51.0 3.2 %fusion.1 = bf16[48,5120]{1,0:T(8,128)(2,1)} fusion(bf16[1,128,5120]{2,1,0:T(8,128)(2,1)} %param.8, bf16[1,128,5120]{2,1,0:T(8,128)(2,1)S(1)} %copy-done, bf16[192,5120]{1,0:T(8,128)(2,1)S(1)} %bitcast_dynamic-update-slice_fusion), kind=kOutput, calls=%fused_computation.5 | convolution fusion | flops 126332928 | bytes 3604480 | tf_op jit(solution)/shard_map/dot_general | solution.py:34
  54.3 3.2 %fusion.2 = bf16[48,5120]{1,0:T(8,128)(2,1)} fusion(bf16[1,128,5120]{2,1,0:T(8,128)(2,1)S(1)} %copy-done, bf16[1,128,5120]{2,1,0:T(8,128)(2,1)} %param.9, bf16[192,5120]{1,0:T(8,128)(2,1)S(1)} %bitcast_dynamic-update-slice_fusion), kind=kOutput, calls=%fused_computation.6 | convolution fusion | flops 126332928 | bytes 3604480 | tf_op jit(solution)/shard_map/dot_general | solution.py:34
  57.4 3.2 %fusion.3 = bf16[48,5120]{1,0:T(8,128)(2,1)} fusion(bf16[1,128,5120]{2,1,0:T(8,128)(2,1)} %param.9, bf16[1,128,5120]{2,1,0:T(8,128)(2,1)S(1)} %copy-done, bf16[192,5120]{1,0:T(8,128)(2,1)S(1)} %bitcast_dynamic-update-slice_fusion), kind=kOutput, calls=%fused_computation.7 | convolution fusion | flops 126332928 | bytes 3604480 | tf_op jit(solution)/shard_map/dot_general | solution.py:34
  60.6 2.9 %pad_maximum_fusion = bf16[192,5120]{1,0:T(8,128)(2,1)} fusion(bf16[48,5120]{1,0:T(8,128)(2,1)} %fusion.3, bf16[48,5120]{1,0:T(8,128)(2,1)} %fusion.2, bf16[48,5120]{1,0:T(8,128)(2,1)} %fusion.1, bf16[48,5120]{1,0:T(8,128)(2,1)} %fusion), kind=kLoop, calls=%fused_computation.8 | loop fusion | flops 7864320 | bytes 3932160 | tf_op jit(solution)/shard_map/concatenate | solution.py:61
  63.5 0.0 copy-start.2
  63.5 0.0 copy-start.3
  63.5 0.0 copy-start.4
  63.5 0.0 copy-start.5
  63.5 0.0 reduce-scatter.2.cloned.1.call-update
  63.6 41.6 %reduce-scatter.2.cloned.1.call-done = bf16[48,5120]{1,0:T(8,128)(2,1)} async-done(((bf16[192,5120]{1,0:T(8,128)(2,1)}), bf16[48,5120]{1,0:T(8,128)(2,1)}) %reduce-scatter.2.cloned.1.call-update) | async-done | bytes 491536 | tf_op jit(solution)/shard_map/reduce_scatter | solution.py:69
  105.1 0.0 copy-done.2
  105.1 0.0 copy-done.3
  105.1 0.0 copy-done.4
  105.1 1.9 %fusion.50 = bf16[48,5120]{1,0:T(8,128)(2,1)S(1)} fusion(bf16[48,5120]{1,0:T(8,128)(2,1)} %reduce-scatter.2.cloned.1.call-done, bf16[1,48,5120]{2,1,0:T(8,128)(2,1)S(1)} %copy-done.3, bf16[1,48,5120]{2,1,0:T(8,128)(2,1)S(1)} %copy-done.4, bf16[1,48,5120]{2,1,0:T(8,128)(2,1)S(1)} %copy-done.2), kind=kLoop, calls=%fused_computation.36 | loop fusion | flops 5160960 | bytes 2457600 | tf_op jit(solution)/shard_map/convert_element_type | solution.py:85
  107.1 2.0 %collective-permute-start.3 = (bf16[48,5120]{1,0:T(8,128)(2,1)S(1)}, bf16[48,5120]{1,0:T(8,128)(2,1)S(1)}, u32[]{:S(2)}, u32[]{:S(2)}) collective-permute-start(bf16[48,5120]{1,0:T(8,128)(2,1)S(1)} %fusion.50), channel_id=1, source_target_pairs={{0,4},{4,8},{8,12},{12,16},{16,20},{20,24},{24,28},{28,0},{1,5},{5... | collective-permute-start | bytes 1474568 | tf_op jit(solution)/shard_map/ppermute | solution.py:29
  109.0 0.0 collective-permute-start.4
  109.0 0.0 copy-done.5
  109.0 0.6 fusion.76
  109.7 8.6 %collective-permute-done.3 = bf16[48,5120]{1,0:T(8,128)(2,1)S(1)} collective-permute-done((bf16[48,5120]{1,0:T(8,128)(2,1)S(1)}, bf16[48,5120]{1,0:T(8,128)(2,1)S(1)}, u32[]{:S(2)}, u32[]{:S(2)}) %collective-permute-start.3) | collective-permute-done | bytes 491552 | tf_op jit(solution)/shard_map/ppermute | solution.py:29
  118.2 3.4 %collective-permute-done.4 = bf16[48,5120]{1,0:T(8,128)(2,1)S(1)} collective-permute-done((bf16[48,5120]{1,0:T(8,128)(2,1)S(1)}, bf16[48,5120]{1,0:T(8,128)(2,1)S(1)}, u32[]{:S(2)}, u32[]{:S(2)}) %collective-permute-start.4) | collective-permute-done | bytes 491552 | tf_op jit(solution)/shard_map/ppermute | solution.py:29
  121.7 2.9 %fusion.59 = bf16[1,48,5120]{2,1,0:T(8,128)(2,1)} fusion(bf16[48,5120]{1,0:T(8,128)(2,1)S(1)} %collective-permute-done.4, bf16[48,5120]{1,0:T(8,128)(2,1)S(1)} %fusion.50, bf16[48,5120]{1,0:T(8,128)(2,1)S(1)} %collective-permute-done.3, f32[]{:T(128)} %bitcast.11, f32[]{:T(128)} %bitcast.10, f32[]{:T(128)} %bitcast), kind=kLoop, calls=%fused_computation.46 | loop fusion | flops 2457600 | bytes 1966092 | tf_op jit(solution)/shard_map/broadcast_in_dim | solution.py:91
  (4 shorter events, 0.1 us)
Async XLA Ops:
  6.5 41.3 %copy-start = (bf16[1,128,5120]{2,1,0:T(8,128)(2,1)S(1)}, bf16[1,128,5120]{2,1,0:T(8,128)(2,1)}, u32[]{:S(2)}) copy-start(bf16[1,128,5120]{2,1,0:T(8,128)(2,1)} %param.7) | copy-start | bytes 3932164
  6.5 98.6 %reduce-scatter.2.cloned.1.call-start = ((), (), s32[]{:S(2)}) async-start(), calls=%async_computation.1 | async-start | bytes 2457600 | tf_op jit(solution)/shard_map/reduce_scatter | solution.py:69
  6.5 15.4 %collective-permute-start = (bf16[1,48,5120]{2,1,0:T(8,128)(2,1)}, bf16[1,48,5120]{2,1,0:T(8,128)(2,1)}, u32[]{:S(2)}, u32[]{:S(2)}) collective-permute-start(bf16[1,48,5120]{2,1,0:T(8,128)(2,1)} %param.10), channel_id=1, source_target_pairs={{0,1},{1,2},{2,3},{3,0},{4,5},{5,6},{6,7},{7,4},{8,9},{9,10},{10,1... | collective-permute-start | bytes 1474568 | tf_op jit(solution)/shard_map/ppermute | solution.py:23
  8.7 1.1 copy-start.1
  22.0 13.5 %collective-permute-start.1 = (bf16[1,48,5120]{2,1,0:T(8,128)(2,1)}, bf16[1,48,5120]{2,1,0:T(8,128)(2,1)S(1)}, u32[]{:S(2)}, u32[]{:S(2)}) collective-permute-start(bf16[1,48,5120]{2,1,0:T(8,128)(2,1)} %collective-permute-done), channel_id=1, source_target_pairs={{0,1},{1,2},{2,3},{3,0},{4,5},{5,6},{6,7},{7,4},{8,9},{9,10},{10,1... | collective-permute-start | bytes 1474568 | tf_op jit(solution)/shard_map/ppermute | solution.py:23
  35.4 12.4 %collective-permute-start.2 = (bf16[1,48,5120]{2,1,0:T(8,128)(2,1)S(1)}, bf16[1,48,5120]{2,1,0:T(8,128)(2,1)S(1)}, u32[]{:S(2)}, u32[]{:S(2)}) collective-permute-start(bf16[1,48,5120]{2,1,0:T(8,128)(2,1)S(1)} %collective-permute-done.1), channel_id=1, source_target_pairs={{0,1},{1,2},{2,3},{3,0},{4,5},{5,6},{6,7},{7,4},{8,9},{9,10},{10,1... | collective-permute-start | bytes 1474568 | tf_op jit(solution)/shard_map/ppermute | solution.py:23
  63.5 41.6 %copy-start.2 = (bf16[1,48,5120]{2,1,0:T(8,128)(2,1)S(1)}, bf16[1,48,5120]{2,1,0:T(8,128)(2,1)}, u32[]{:S(2)}) copy-start(bf16[1,48,5120]{2,1,0:T(8,128)(2,1)} %param.10) | copy-start | bytes 1474564
  63.5 41.6 %copy-start.3 = (bf16[1,48,5120]{2,1,0:T(8,128)(2,1)S(1)}, bf16[1,48,5120]{2,1,0:T(8,128)(2,1)}, u32[]{:S(2)}) copy-start(bf16[1,48,5120]{2,1,0:T(8,128)(2,1)} %param.12) | copy-start | bytes 1474564
  63.5 41.6 %copy-start.4 = (bf16[1,48,5120]{2,1,0:T(8,128)(2,1)S(1)}, bf16[1,48,5120]{2,1,0:T(8,128)(2,1)}, u32[]{:S(2)}) copy-start(bf16[1,48,5120]{2,1,0:T(8,128)(2,1)} %param.11) | copy-start | bytes 1474564
  63.5 45.5 %copy-start.5 = (s32[1,3]{1,0:T(1,128)S(1)}, s32[1,3]{1,0:T(1,128)}, u32[]{:S(2)}) copy-start(s32[1,3]{1,0:T(1,128)} %param.13) | copy-start | bytes 40
  107.1 11.2 %collective-permute-start.3 = (bf16[48,5120]{1,0:T(8,128)(2,1)S(1)}, bf16[48,5120]{1,0:T(8,128)(2,1)S(1)}, u32[]{:S(2)}, u32[]{:S(2)}) collective-permute-start(bf16[48,5120]{1,0:T(8,128)(2,1)S(1)} %fusion.50), channel_id=1, source_target_pairs={{0,4},{4,8},{8,12},{12,16},{16,20},{20,24},{24,28},{28,0},{1,5},{5... | collective-permute-start | bytes 1474568 | tf_op jit(solution)/shard_map/ppermute | solution.py:29
  109.0 12.7 %collective-permute-start.4 = (bf16[48,5120]{1,0:T(8,128)(2,1)S(1)}, bf16[48,5120]{1,0:T(8,128)(2,1)S(1)}, u32[]{:S(2)}, u32[]{:S(2)}) collective-permute-start(bf16[48,5120]{1,0:T(8,128)(2,1)S(1)} %fusion.50), channel_id=1, source_target_pairs={{0,28},{4,0},{8,4},{12,8},{16,12},{20,16},{24,20},{28,24},{1,29},{... | collective-permute-start | bytes 1474568 | tf_op jit(solution)/shard_map/ppermute | solution.py:29
Sparse Core Ops, SparseCore 0:
  63.7 41.3 reduce-scatter.1
